TPU v7x, 32 devices: a whole 2x2x4 slice. The times are simulated.
32 devices in a mesh: beam: 2 (over x), band: 2 (over core), tm: 8 (over z, y).
Axes of the slice: x: 2, y: 2, z: 4, core: 2. Of those that a mesh axis runs over, the one named last changes fastest.
Arguments:
- samples: bfloat16 [2048, 32768], P(('beam', 'band'), 'tm'), parts along dimension 0, may hold values from -3 to 3
- clip_mask: int32 [2048, 256], P(('beam', 'band'), 'tm'), parts along dimension 0, may hold values 0 or 1
- delays: int32 [8, 1024], P(None, 'band'), may hold values from 0 to 4095
- templates: bfloat16 [2, 64, 1024], replicated, may hold values from -0.125 to 0.125
Outputs:
- powers: float32 [16, 64, 16384], P(('beam', 'tm'), None, 'band'), parts along dimension 0
There are 2 independent parts, one for each index of `beam`. A program takes and returns all parts, laid end to end along the dimension named above; an argument that names none is the same for every part. Nothing has to cross between parts.
All inputs are finite; a program needn't handle non-finite values. No bound on the sum of `clip_mask` on one device may be relied on, other than what follows from the above.
Results may differ from a plain program's by a relative error of at most 0.0095.
Values may be sent and summed in bfloat16 or wider, within the bound.
A program may use at most 192 MiB of HBM per device.

v0:
```python
import math

import jax
import jax.numpy as jnp
from jax import lax
from jax.experimental import pallas as pl
from jax.experimental.pallas import tpu as pltpu
from jax.sharding import PartitionSpec as P

CHANNELS = 1024
SEARCH = 16384
LANES = 128

clip_level = 2.5
highest = lax.Precision.HIGHEST


def counting(length):
    return jnp.arange(length, dtype=jnp.int32)


def phase_table(first_index, second_index, period):
    turn_count = first_index[:, None] * second_index[None, :] % period
    angles = turn_count.astype(jnp.float32) * (2.0 * math.pi / period)
    return (jnp.cos(angles), jnp.sin(angles))


def dedisperse(samples, clip_mask, delays):
    chan_count, slab_len = samples.shape
    rows = slab_len // LANES
    dm_count = delays.shape[0]
    block = 64
    steps = chan_count // block
    padded_len = 2 * slab_len
    scale = 1.0 / math.sqrt(CHANNELS)

    def kernel(delay_ref, sample_ref, mask_ref, out_ref, wrapped_ref, total_ref):
        step = pl.program_id(0)

        @pl.when(step == 0)
        def _():
            total_ref[...] = jnp.zeros_like(total_ref)

        for group in range(block // 16):
            picked = pl.ds(group * 16, 16)
            flags = mask_ref[picked, :].astype(jnp.float32)
            for row in range(rows):
                values = sample_ref[picked, row * LANES : (row + 1) * LANES].astype(jnp.float32)
                values = jnp.clip(values, -clip_level, clip_level) * flags[:, row : row + 1]
                wrapped_ref[picked, row, :] = values
                wrapped_ref[picked, row + rows, :] = values

        lane = lax.broadcasted_iota(jnp.int32, (rows, LANES), 1)
        index = lax.broadcasted_iota(jnp.int32, (rows, LANES), 0) * LANES + lane

        def one_dm(dm, _):
            def one_channel(chan, sums):
                both, own = sums
                delay = delay_ref[dm, step * block + chan]
                high = delay // LANES
                low = delay % LANES
                same = wrapped_ref[chan, pl.ds(rows - high, rows), :]
                before = wrapped_ref[chan, pl.ds(rows - 1 - high, rows), :]
                moved = pltpu.roll(jnp.where(lane < LANES - low, same, before), low, 1)
                return (both + moved, own + jnp.where(index >= delay, moved, 0.0))

            both, own = lax.fori_loop(
                0, block, one_channel, (total_ref[dm, 0], total_ref[dm, 1]), unroll=8
            )
            total_ref[dm, 0] = both
            total_ref[dm, 1] = own
            return 0

        lax.fori_loop(0, dm_count, one_dm, 0)

        @pl.when(step == steps - 1)
        def _():
            sign = (1 - 2 * (lane % 2)).astype(jnp.float32)

            def finish(dm, _):
                both = total_ref[dm, 0]
                own = total_ref[dm, 1]
                half_rate = jnp.sum(both * sign) * sign * (1.0 / padded_len)
                out_ref[dm, :rows, :] = (own - half_rate) * scale
                out_ref[dm, rows:, :] = (both - own - half_rate) * scale
                return 0

            lax.fori_loop(0, dm_count, finish, 0)

    return pl.pallas_call(
        kernel,
        out_shape=jax.ShapeDtypeStruct((dm_count, 2 * rows, LANES), jnp.float32),
        grid_spec=pltpu.PrefetchScalarGridSpec(
            num_scalar_prefetch=1,
            grid=(steps,),
            in_specs=[
                pl.BlockSpec((block, slab_len), lambda i, *_: (i, 0)),
                pl.BlockSpec((block, clip_mask.shape[1]), lambda i, *_: (i, 0)),
            ],
            out_specs=pl.BlockSpec((dm_count, 2 * rows, LANES), lambda i, *_: (0, 0, 0)),
            scratch_shapes=[
                pltpu.VMEM((block, 2 * rows, LANES), jnp.float32),
                pltpu.VMEM((dm_count, 2, rows, LANES), jnp.float32),
            ],
        ),
        compiler_params=pltpu.CompilerParams(vmem_limit_bytes=48 << 20),
    )(delays, samples, clip_mask)


def correlate(framed, templates, bin_count):
    tmpl_count, tap_len = templates.shape[1:]
    blocks = tap_len // LANES
    frame_len = framed.shape[1]
    width = 1024
    steps = bin_count // width

    def kernel(framed_ref, tmpl_ref, out_ref, taps_ref, shifted_ref):
        step = pl.program_id(0)

        @pl.when(step == 0)
        def _():
            row = lax.broadcasted_iota(jnp.int32, (LANES, LANES), 0)
            col = lax.broadcasted_iota(jnp.int32, (LANES, LANES), 1)
            flip = (row + col == LANES - 1).astype(jnp.bfloat16)
            for b in range(blocks):
                cut = slice(b * LANES, (b + 1) * LANES)
                real = jnp.dot(tmpl_ref[0, :, cut], flip, preferred_element_type=jnp.float32)
                imag = jnp.dot(tmpl_ref[1, :, cut], flip, preferred_element_type=jnp.float32)
                taps_ref[b, :tmpl_count, :LANES] = real.astype(jnp.bfloat16)
                taps_ref[b, :tmpl_count, LANES:] = (-imag).astype(jnp.bfloat16)
                taps_ref[b, tmpl_count:, :LANES] = imag.astype(jnp.bfloat16)
                taps_ref[b, tmpl_count:, LANES:] = real.astype(jnp.bfloat16)
            for part in range(2):
                spread = jnp.broadcast_to(framed_ref[part : part + 1, :], (8, frame_len))
                base = pltpu.roll(spread, 0, 1, stride=1, stride_axis=0)
                for g in range(LANES // 16):
                    lower = base if g == 0 else pltpu.roll(base, 16 * g, 1)
                    upper = pltpu.roll(base, 16 * g + 8, 1)
                    start = part * LANES + 16 * g
                    shifted_ref[start : start + 16, :] = jnp.concatenate(
                        [lower, upper], axis=0
                    ).astype(jnp.bfloat16)

        total = jnp.zeros((2 * tmpl_count, width), jnp.float32)
        for b in range(blocks):
            first = pl.multiple_of(step * width + (b + 1) * LANES, LANES)
            total = total + jnp.dot(
                taps_ref[b], shifted_ref[:, pl.ds(first, width)], preferred_element_type=jnp.float32
            )
        out_ref[0] = jnp.square(total[:tmpl_count]) + jnp.square(total[tmpl_count:])

    return pl.pallas_call(
        kernel,
        out_shape=jax.ShapeDtypeStruct((1, tmpl_count, bin_count), jnp.float32),
        grid=(steps,),
        in_specs=[
            pl.BlockSpec((2, frame_len), lambda i: (0, 0)),
            pl.BlockSpec(templates.shape, lambda i: (0, 0, 0)),
        ],
        out_specs=pl.BlockSpec((1, tmpl_count, width), lambda i: (0, 0, i)),
        scratch_shapes=[
            pltpu.VMEM((blocks, 2 * tmpl_count, 2 * LANES), jnp.bfloat16),
            pltpu.VMEM((2 * LANES, frame_len), jnp.bfloat16),
        ],
        compiler_params=pltpu.CompilerParams(vmem_limit_bytes=48 << 20),
    )(framed, templates)


def local(samples, clip_mask, delays, templates):
    partial_value = dedisperse(samples, clip_mask, delays)
    first_bins = partial_value.shape[1]
    half_rows = first_bins // 2
    inner_len = LANES
    owned = lax.all_to_all(partial_value, "tm", split_axis=0, concat_axis=1, tiled=True)
    slab_count = owned.shape[1] // first_bins
    paired = owned.reshape(slab_count, 2, half_rows, inner_len)
    carried = jnp.concatenate(
        [jnp.zeros((1, half_rows, inner_len), jnp.float32), paired[:-1, 1]], axis=0
    )
    series = (paired[:, 0] + carried).reshape(slab_count * half_rows, inner_len)
    whole = lax.psum(series, "band")
    return search(whole, templates)


def search(whole, templates):
    row_count, inner_len = whole.shape
    total_len = row_count * inner_len
    bin_cols = SEARCH // row_count
    scale_bins = 1.0 / math.sqrt(total_len)
    outer_cos, outer_sin = phase_table(counting(row_count), counting(row_count), row_count)
    table_outer = jnp.concatenate([outer_cos, -outer_sin], axis=0)
    hold_cos, hold_sin = phase_table(counting(row_count), counting(inner_len), total_len)
    own_cols = bin_cols // lax.axis_size("band")
    folded = jnp.dot(table_outer, whole, precision=highest)
    fold_real = folded[:row_count]
    fold_imag = folded[row_count:]
    hold_real = fold_real * hold_cos + fold_imag * hold_sin
    hold_imag = fold_imag * hold_cos - fold_real * hold_sin
    half_taps = templates.shape[2] // 2
    side_cols = -(-half_taps // row_count)
    cols = lax.axis_index("band") * own_cols - side_cols + counting(own_cols + 2 * side_cols)
    last_cos, last_sin = phase_table(counting(inner_len), cols % inner_len, inner_len)
    inside = ((cols >= 0) & (cols < bin_cols)).astype(jnp.float32) * scale_bins
    last_cos = last_cos * inside
    last_sin = last_sin * inside
    table_last = jnp.concatenate(
        [
            jnp.concatenate([last_cos, -last_sin], axis=1),
            jnp.concatenate([last_sin, last_cos], axis=1),
        ],
        axis=0,
    )
    out = jnp.dot(jnp.concatenate([hold_real, hold_imag], axis=1), table_last, precision=highest)
    ordered = out.T.reshape(2, -1)
    local_bins = own_cols * row_count
    skip = side_cols * row_count - half_taps
    if skip:
        framed = ordered[:, skip - 1 : skip - 1 + local_bins + 2 * half_taps]
    else:
        framed = jnp.pad(ordered[:, :-1], ((0, 0), (1, 0)))
    return correlate(framed, templates, local_bins)


def solution(mesh):
    in_specs = (P(("beam", "band"), "tm"), P(("beam", "band"), "tm"), P(None, "band"), P())
    out_specs = P(("beam", "tm"), None, "band")
    return jax.shard_map(local, mesh=mesh, in_specs=in_specs, out_specs=out_specs, check_vma=False)
```

profile of v0, /device:TPU:0, one launch (start us, length us, event | category | flops | bytes accessed | tf_op | source)
XLA Modules:
  0.0 149.4 jit_solution(6126497366851041652)
XLA Ops:
  6.5 1.0 copy.7.mask_ref
  7.5 0.0 copy-start
  7.5 2.2 %copy-done = bf16[512,4096]{1,0:T(8,128)(2,1)S(1)} copy-done((bf16[512,4096]{1,0:T(8,128)(2,1)S(1)}, bf16[512,4096]{1,0:T(8,128)(2,1)}, u32[]{:S(2)}) %copy-start) | copy-done | bytes 4194328
  9.7 0.0 copy-start.2
  9.7 0.7 copy-done.2
  10.4 0.0 copy-start.1
  10.4 87.1 %shard_map.46 = f32[8,64,128]{2,1,0:T(8,128)} custom-call(s32[8,512]{1,0:T(8,128)S(1)} %copy-done.2, bf16[512,4096]{1,0:T(8,128)(2,1)S(1)} %copy-done, s32[512,32]{1,0:T(8,128)S(1)} %copy.7.mask_ref), custom_call_target="tpu_custom_call" | custom-call | tf_op jit(solution)/shard_map/pallas_call | solution.py:90
  97.5 7.3 %all-to-all-start = ((f32[8,64,128]{2,1,0:T(8,128)}), f32[8,64,128]{2,1,0:T(8,128)S(1)}, u32[]{:S(2)}, u32[]{:S(2)}) async-start(f32[8,64,128]{2,1,0:T(8,128)} %shard_map.46), calls=%async_computation | async-start | bytes 524288 | tf_op jit(solution)/shard_map/all_to_all | solution.py:174
  104.8 0.0 all-reduce.4.cloned.1.call-start
  104.9 8.8 %all-to-all-done = f32[8,64,128]{2,1,0:T(8,128)S(1)} async-done(((f32[8,64,128]{2,1,0:T(8,128)}), f32[8,64,128]{2,1,0:T(8,128)S(1)}, u32[]{:S(2)}, u32[]{:S(2)}) %all-to-all-start) | async-done | bytes 262176 | tf_op jit(solution)/shard_map/all_to_all | solution.py:174
  113.8 0.7 fusion.17
  114.4 0.0 all-reduce.4.cloned.1.call-update
  114.5 0.2 fusion.37
  114.6 1.0 sine_negate_fusion
  115.7 15.9 %all-reduce.4.cloned.1.call-done = f32[256,128]{1,0:T(8,128)} async-done(((f32[256,128]{1,0:T(8,128)}), f32[256,128]{1,0:T(8,128)}) %all-reduce.4.cloned.1.call-update) | async-done | bytes 131088 | tf_op jit(solution)/shard_map/psum | solution.py:181
  131.5 1.6 %fusion = f32[512,128]{0,1:T(8,128)S(1)} fusion(f32[256,128]{1,0:T(8,128)} %all-reduce.4.cloned.1.call-done, f32[256,256]{1,0:T(8,128)S(1)} %get-tuple-element.10, f32[256,256]{1,0:T(8,128)S(1)} %get-tuple-element.11), kind=kOutput, calls=%fused_computation | convolution fusion | flops 201457664 | bytes 917504 | tf_op jit(solution)/shard_map/dot_general | solution.py:194
  133.1 0.6 multiply_add_fusion
  133.7 0.3 fusion.7
  134.0 0.1 pad.5.framed_ref
  134.1 0.0 copy-done.1
  134.2 8.4 %shard_map.47 = f32[1,64,8192]{2,1,0:T(8,128)} custom-call(f32[2,9216]{1,0:T(2,128)S(1)} %pad.5.framed_ref, bf16[2,64,1024]{2,1,0:T(8,128)(2,1)S(1)} %copy-done.1), custom_call_target="tpu_custom_call" | custom-call | tf_op jit(solution)/shard_map/pallas_call | solution.py:152
  (4 shorter events, 0.1 us)
Async XLA Ops:
  7.5 2.2 %copy-start = (bf16[512,4096]{1,0:T(8,128)(2,1)S(1)}, bf16[512,4096]{1,0:T(8,128)(2,1)}, u32[]{:S(2)}) copy-start(bf16[512,4096]{1,0:T(8,128)(2,1)} %sample_ref.1) | copy-start | bytes 12582916
  9.7 0.7 copy-start.2
  10.4 123.7 %copy-start.1 = (bf16[2,64,1024]{2,1,0:T(8,128)(2,1)S(1)}, bf16[2,64,1024]{2,1,0:T(8,128)(2,1)}, u32[]{:S(2)}) copy-start(bf16[2,64,1024]{2,1,0:T(8,128)(2,1)} %tmpl_ref.1) | copy-start | bytes 786436
  97.5 16.2 %all-to-all-start = ((f32[8,64,128]{2,1,0:T(8,128)}), f32[8,64,128]{2,1,0:T(8,128)S(1)}, u32[]{:S(2)}, u32[]{:S(2)}) async-start(f32[8,64,128]{2,1,0:T(8,128)} %shard_map.46), calls=%async_computation | async-start | bytes 524288 | tf_op jit(solution)/shard_map/all_to_all | solution.py:174
  104.8 26.7 %all-reduce.4.cloned.1.call-start = ((), (), s32[]{:S(2)}) async-start(), calls=%async_computation.1 | async-start | bytes 262144 | tf_op jit(solution)/shard_map/psum | solution.py:181
Sparse Core Ops, SparseCore 0:
  114.6 16.9 all-reduce.3
where the time goes:
time: 150 us; the launch traced here: 149 us
  Pallas kernels  95.5 us (64%)
  waiting for transfers between devices  24.7 us (16%)
  between operations  13.5 us (9%)
  starting transfers between devices  7.35 us (5%)
  local copies, waits for them, and re-layouts  4.06 us (3%)
  other arithmetic  2.46 us (2%)
  matrix products  1.84 us (1%)
    pallas_call x1, Pallas kernels, dedisperse(): pl.pallas_call(kernel, out_shape=jax.ShapeDtypeStruct((dm_count, 2 * rows...  87.1 us
    psum x1, waiting for transfers between devices, local(): whole = lax.psum(series, 'band')  15.9 us
    all_to_all x1, waiting for transfers between devices, local(): lax.all_to_all(partial_value, 'tm', split_axis=0, concat_axis=1, tiled=True)  8.84 us
    pallas_call x1, Pallas kernels, correlate(): pl.pallas_call(kernel, out_shape=jax.ShapeDtypeStruct((1, tmpl_count, bin...  8.41 us
    all_to_all x1, starting transfers between devices, local(): lax.all_to_all(partial_value, 'tm', split_axis=0, concat_axis=1, tiled=True)  7.31 us
    unnamed x7, local copies, waits for them, and re-layouts  3.87 us
  transfers between devices with their start and end apart: 2, of which 2 were waited for; matrix products, arithmetic and copies ran while one was open for 1% of the time, Pallas kernels for 0%

commit v1 on v0

--- a/solution.py
+++ b/solution.py
@@ -33,6 +33,7 @@
     steps = chan_count // block
     padded_len = 2 * slab_len
     scale = 1.0 / math.sqrt(CHANNELS)
+    lane_bits = LANES.bit_length() - 1
 
     def kernel(delay_ref, sample_ref, mask_ref, out_ref, wrapped_ref, total_ref):
         step = pl.program_id(0)
@@ -47,28 +48,50 @@
             for row in range(rows):
                 values = sample_ref[picked, row * LANES : (row + 1) * LANES].astype(jnp.float32)
                 values = jnp.clip(values, -clip_level, clip_level) * flags[:, row : row + 1]
-                wrapped_ref[picked, row, :] = values
-                wrapped_ref[picked, row + rows, :] = values
+                for half in range(2):
+                    part = values[8 * half : 8 * half + 8]
+                    first = (group * 16 + 8 * half) * 2 * rows + row
+                    wrapped_ref[pl.ds(first, 8, stride=2 * rows), :] = part
+                    wrapped_ref[pl.ds(first + rows, 8, stride=2 * rows), :] = part
 
         lane = lax.broadcasted_iota(jnp.int32, (rows, LANES), 1)
         index = lax.broadcasted_iota(jnp.int32, (rows, LANES), 0) * LANES + lane
+        from_end = LANES - 1 - lane[:8]
 
         def one_dm(dm, _):
+            chan_base = dm * chan_count + step * block
+
             def one_channel(chan, sums):
                 both, own = sums
-                delay = delay_ref[dm, step * block + chan]
-                high = delay // LANES
-                low = delay % LANES
-                same = wrapped_ref[chan, pl.ds(rows - high, rows), :]
-                before = wrapped_ref[chan, pl.ds(rows - 1 - high, rows), :]
-                moved = pltpu.roll(jnp.where(lane < LANES - low, same, before), low, 1)
-                return (both + moved, own + jnp.where(index >= delay, moved, 0.0))
-
+                delay = delay_ref[chan_base + chan]
+                low = delay & (LANES - 1)
+                start = chan * (2 * rows) + (rows - 1) - (delay >> lane_bits)
+                keep = from_end >= low
+                new_both, new_own = [], []
+                for r in range(rows // 8):
+                    same = wrapped_ref[pl.ds(start + (1 + 8 * r), 8), :]
+                    before = wrapped_ref[pl.ds(start + 8 * r, 8), :]
+                    moved = pltpu.roll(jnp.where(keep, same, before), low, 1)
+                    new_both.append(both[r] + moved)
+                    new_own.append(
+                        own[r] + jnp.where(index[8 * r : 8 * r + 8] >= delay, moved, 0.0)
+                    )
+                return (tuple(new_both), tuple(new_own))
+
+            tiles = [slice(8 * r, 8 * r + 8) for r in range(rows // 8)]
             both, own = lax.fori_loop(
-                0, block, one_channel, (total_ref[dm, 0], total_ref[dm, 1]), unroll=8
-            )
-            total_ref[dm, 0] = both
-            total_ref[dm, 1] = own
+                0,
+                block,
+                one_channel,
+                (
+                    tuple(total_ref[dm, 0, t, :] for t in tiles),
+                    tuple(total_ref[dm, 1, t, :] for t in tiles),
+                ),
+                unroll=64,
+            )
+            for t, x, y in zip(tiles, both, own):
+                total_ref[dm, 0, t, :] = x
+                total_ref[dm, 1, t, :] = y
             return 0
 
         lax.fori_loop(0, dm_count, one_dm, 0)
@@ -81,15 +104,15 @@
                 both = total_ref[dm, 0]
                 own = total_ref[dm, 1]
                 half_rate = jnp.sum(both * sign) * sign * (1.0 / padded_len)
-                out_ref[dm, :rows, :] = (own - half_rate) * scale
-                out_ref[dm, rows:, :] = (both - own - half_rate) * scale
+                out_ref[dm, :rows, :] = ((own - half_rate) * scale).astype(out_ref.dtype)
+                out_ref[dm, rows:, :] = ((both - own - half_rate) * scale).astype(out_ref.dtype)
                 return 0
 
             lax.fori_loop(0, dm_count, finish, 0)
 
     return pl.pallas_call(
         kernel,
-        out_shape=jax.ShapeDtypeStruct((dm_count, 2 * rows, LANES), jnp.float32),
+        out_shape=jax.ShapeDtypeStruct((dm_count, 2 * rows, LANES), jnp.bfloat16),
         grid_spec=pltpu.PrefetchScalarGridSpec(
             num_scalar_prefetch=1,
             grid=(steps,),
@@ -99,12 +122,103 @@
             ],
             out_specs=pl.BlockSpec((dm_count, 2 * rows, LANES), lambda i, *_: (0, 0, 0)),
             scratch_shapes=[
-                pltpu.VMEM((block, 2 * rows, LANES), jnp.float32),
+                pltpu.VMEM((block * 2 * rows, LANES), jnp.float32),
                 pltpu.VMEM((dm_count, 2, rows, LANES), jnp.float32),
             ],
         ),
         compiler_params=pltpu.CompilerParams(vmem_limit_bytes=48 << 20),
-    )(delays, samples, clip_mask)
+    )(delays.reshape(-1), samples, clip_mask)
+
+
+def gather_series(partial_value):
+    tm_count = lax.axis_size("tm")
+    band_count = lax.axis_size("band")
+    _, padded_rows, _ = partial_value.shape
+    rows = padded_rows // 2
+    mesh_ids = pl.DeviceIdType.MESH
+
+    def kernel(part_ref, out_ref, held_ref, sent, arrived, passed, received, local_sem):
+        me = lax.axis_index("tm")
+        band = lax.axis_index("band")
+
+        def device(tm, core):
+            return {"tm": tm, "band": core}
+
+        barrier = pltpu.get_barrier_semaphore()
+        for k in range(1, tm_count):
+            pl.semaphore_signal(
+                barrier, 1, device_id=device(lax.rem(me + k, tm_count), band), device_id_type=mesh_ids
+            )
+        for j in range(1, band_count):
+            pl.semaphore_signal(
+                barrier, 1, device_id=device(me, lax.rem(band + j, band_count)), device_id_type=mesh_ids
+            )
+        pl.semaphore_wait(barrier, tm_count + band_count - 2)
+
+        outgoing = []
+        for k in range(1, tm_count):
+            target = lax.rem(me + k, tm_count)
+            copy = pltpu.make_async_remote_copy(
+                src_ref=part_ref.at[target],
+                dst_ref=held_ref.at[band, me],
+                send_sem=sent.at[k],
+                recv_sem=arrived.at[k],
+                device_id=device(target, band),
+                device_id_type=mesh_ids,
+            )
+            copy.start()
+            outgoing.append(copy)
+        kept = pltpu.make_async_copy(part_ref.at[me], held_ref.at[band, me], local_sem)
+        kept.start()
+        handed = []
+
+        def hand_on(source, piece, slot):
+            for j in range(1, band_count):
+                copy = pltpu.make_async_remote_copy(
+                    src_ref=piece,
+                    dst_ref=held_ref.at[band, source],
+                    send_sem=passed.at[slot, j],
+                    recv_sem=received.at[slot, j],
+                    device_id=device(me, lax.rem(band + j, band_count)),
+                    device_id_type=mesh_ids,
+                )
+                copy.start()
+                handed.append(copy)
+
+        hand_on(me, part_ref.at[me], 0)
+        for k in range(1, tm_count):
+            outgoing[k - 1].wait_recv()
+            source = lax.rem(me + tm_count - k, tm_count)
+            hand_on(source, held_ref.at[band, source], k)
+        for copy in outgoing:
+            copy.wait_send()
+        kept.wait()
+        for copy in handed:
+            copy.wait()
+
+        tail = jnp.zeros((rows, LANES), jnp.float32)
+        for s in range(tm_count):
+            piece = held_ref[0, s].astype(jnp.float32)
+            for b in range(1, band_count):
+                piece = piece + held_ref[b, s].astype(jnp.float32)
+            out_ref[s * rows : (s + 1) * rows, :] = piece[:rows] + tail
+            tail = piece[rows:]
+
+    return pl.pallas_call(
+        kernel,
+        out_shape=jax.ShapeDtypeStruct((tm_count * rows, LANES), jnp.float32),
+        in_specs=[pl.BlockSpec(memory_space=pltpu.VMEM)],
+        out_specs=pl.BlockSpec(memory_space=pltpu.VMEM),
+        scratch_shapes=[
+            pltpu.VMEM((band_count, tm_count, padded_rows, LANES), jnp.bfloat16),
+            pltpu.SemaphoreType.DMA((tm_count,)),
+            pltpu.SemaphoreType.DMA((tm_count,)),
+            pltpu.SemaphoreType.DMA((tm_count, band_count)),
+            pltpu.SemaphoreType.DMA((tm_count, band_count)),
+            pltpu.SemaphoreType.DMA,
+        ],
+        compiler_params=pltpu.CompilerParams(collective_id=0, has_side_effects=True),
+    )(partial_value)
 
 
 def correlate(framed, templates, bin_count):
@@ -168,17 +282,7 @@
 
 def local(samples, clip_mask, delays, templates):
     partial_value = dedisperse(samples, clip_mask, delays)
-    first_bins = partial_value.shape[1]
-    half_rows = first_bins // 2
-    inner_len = LANES
-    owned = lax.all_to_all(partial_value, "tm", split_axis=0, concat_axis=1, tiled=True)
-    slab_count = owned.shape[1] // first_bins
-    paired = owned.reshape(slab_count, 2, half_rows, inner_len)
-    carried = jnp.concatenate(
-        [jnp.zeros((1, half_rows, inner_len), jnp.float32), paired[:-1, 1]], axis=0
-    )
-    series = (paired[:, 0] + carried).reshape(slab_count * half_rows, inner_len)
-    whole = lax.psum(series, "band")
+    whole = gather_series(partial_value)
     return search(whole, templates)
 
 

time: 150 us -> 73.9 us (0.49)
  Pallas kernels: 95.5 us -> 65.2 us
  waiting for transfers between devices: 24.7 us -> 0 us
  between operations: 13.5 us -> 0.09 us
  starting transfers between devices: 7.35 us -> 0 us
    pallas_call x1, Pallas kernels: 87.1 us -> 44.6 us  [dedisperse(): pl.pallas_call(kernel, out_shape=jax.ShapeDtypeStruct((dm_count, 2 * rows...]
    psum x1 -> x0, waiting for transfers between devices: 15.9 us -> none  [local(): whole = lax.psum(series, 'band')]
    pallas_call x0 -> x1, Pallas kernels: none -> 12.2 us  [gather_series(): pl.pallas_call(kernel, out_shape=jax.ShapeDtypeStruct((tm_count * rows, L...]
    all_to_all x1 -> x0, waiting for transfers between devices: 8.84 us -> none  [local(): lax.all_to_all(partial_value, 'tm', split_axis=0, concat_axis=1, tiled=True)]
    all_to_all x1 -> x0, starting transfers between devices: 7.31 us -> none  [local(): lax.all_to_all(partial_value, 'tm', split_axis=0, concat_axis=1, tiled=True)]
    unnamed x7 -> x8, local copies, waits for them, and re-layouts: 3.87 us -> 4.57 us
  transfers between devices with their start and end apart: 2 -> 0, of which waited for: 2 -> 0; matrix products, arithmetic and copies ran while one was open for 1% -> 0% of each run, Pallas kernels for 0% -> 0%
where the time goes in v1:
time: 73.9 us; the launch traced here: 73.7 us
  Pallas kernels  65.2 us (88%)
  local copies, waits for them, and re-layouts  4.75 us (6%)
  matrix products  1.85 us (3%)
  other arithmetic  1.78 us (2%)
    pallas_call x1, Pallas kernels, dedisperse(): pl.pallas_call(kernel, out_shape=jax.ShapeDtypeStruct((dm_count, 2 * rows...  44.6 us
    pallas_call x1, Pallas kernels, gather_series(): pl.pallas_call(kernel, out_shape=jax.ShapeDtypeStruct((tm_count * rows, L...  12.2 us
    pallas_call x1, Pallas kernels, correlate(): pl.pallas_call(kernel, out_shape=jax.ShapeDtypeStruct((1, tmpl_count, bin...  8.41 us
    unnamed x8, local copies, waits for them, and re-layouts  4.57 us
    dot_general x1, matrix products, search(): folded = jnp.dot(table_outer, whole, precision=highest)  1.6 us

profile of v1, /device:TPU:0, one launch (start us, length us, event | category | flops | bytes accessed | tf_op | source)
XLA Modules:
  0.0 73.7 jit_solution(16309589305593283876)
XLA Ops:
  0.0 0.0 copy-start.2
  0.0 0.8 %copy.7 = s32[1,4,8,128]{3,1,2,0:T(4,128)S(1)} copy(s32[1,4,8,128]{3,2,1,0:T(8,128)} %bitcast.6) | data formatting | bytes 32768
  0.8 0.2 fusion.36
  0.9 1.0 %copy.6.mask_ref = s32[512,32]{1,0:T(8,128)S(1)} copy(s32[512,32]{0,1:T(8,128)} %param.5) | data formatting | bytes 131072 | tf_op args[1]
  1.9 0.0 copy-start
  1.9 2.2 %copy-done = bf16[512,4096]{1,0:T(8,128)(2,1)S(1)} copy-done((bf16[512,4096]{1,0:T(8,128)(2,1)S(1)}, bf16[512,4096]{1,0:T(8,128)(2,1)}, u32[]{:S(2)}) %copy-start) | copy-done | bytes 4194328
  4.1 44.6 %shard_map.46.part_ref = bf16[8,64,128]{2,1,0:T(8,128)(2,1)S(1)} custom-call(s32[4096]{0:T(1024)S(1)} %bitcast.4, bf16[512,4096]{1,0:T(8,128)(2,1)S(1)} %copy-done, s32[512,32]{1,0:T(8,128)S(1)} %copy.6.mask_ref), custom_call_target="tpu_custom_call" | custom-call | tf_op jit(solution)/shard_map/pallas_call | solution.py:113
  48.7 0.0 copy-start.1
  48.7 0.6 copy-done.1
  49.4 12.2 %shard_map.47 = f32[256,128]{1,0:T(8,128)} custom-call(bf16[8,64,128]{2,1,0:T(8,128)(2,1)} %copy-done.1), custom_call_target="tpu_custom_call" | custom-call | tf_op jit(solution)/shard_map/pallas_call | solution.py:207
  61.6 1.0 %sine_negate_fusion = (f32[256,256]{1,0:T(8,128)S(1)}, f32[256,256]{1,0:T(8,128)S(1)}) fusion(), kind=kLoop, calls=%fused_computation.14 | loop fusion | flops 983040 | bytes 524288 | tf_op jit(solution)/shard_map/neg | solution.py:295
  62.6 1.6 %fusion = f32[512,128]{0,1:T(8,128)S(1)} fusion(f32[256,128]{1,0:T(8,128)} %shard_map.47, f32[256,256]{1,0:T(8,128)S(1)} %get-tuple-element.10, f32[256,256]{1,0:T(8,128)S(1)} %get-tuple-element.11), kind=kOutput, calls=%fused_computation | convolution fusion | flops 201457664 | bytes 917504 | tf_op jit(solution)/shard_map/dot_general | solution.py:298
  64.2 0.6 multiply_add_fusion
  64.8 0.3 fusion.7
  65.1 0.1 pad.4.framed_ref
  65.2 0.0 copy-done.2
  65.2 8.4 %shard_map.48 = f32[1,64,8192]{2,1,0:T(8,128)} custom-call(f32[2,9216]{1,0:T(2,128)S(1)} %pad.4.framed_ref, bf16[2,64,1024]{2,1,0:T(8,128)(2,1)S(1)} %copy-done.2), custom_call_target="tpu_custom_call" | custom-call | tf_op jit(solution)/shard_map/pallas_call | solution.py:266
  (3 shorter events, 0.1 us)
Async XLA Ops:
  0.0 65.2 %copy-start.2 = (bf16[2,64,1024]{2,1,0:T(8,128)(2,1)S(1)}, bf16[2,64,1024]{2,1,0:T(8,128)(2,1)}, u32[]{:S(2)}) copy-start(bf16[2,64,1024]{2,1,0:T(8,128)(2,1)} %tmpl_ref.1) | copy-start | bytes 786436
  1.9 2.2 %copy-start = (bf16[512,4096]{1,0:T(8,128)(2,1)S(1)}, bf16[512,4096]{1,0:T(8,128)(2,1)}, u32[]{:S(2)}) copy-start(bf16[512,4096]{1,0:T(8,128)(2,1)} %sample_ref.1) | copy-start | bytes 12582916
  48.7 0.7 copy-start.1

commit v2 on v1

--- a/solution.py
+++ b/solution.py
@@ -29,10 +29,11 @@
     chan_count, slab_len = samples.shape
     rows = slab_len // LANES
     dm_count = delays.shape[0]
-    block = 64
+    block = 128
     steps = chan_count // block
     padded_len = 2 * slab_len
     scale = 1.0 / math.sqrt(CHANNELS)
+    assert clip_mask.shape[1] == rows
     lane_bits = LANES.bit_length() - 1
 
     def kernel(delay_ref, sample_ref, mask_ref, out_ref, wrapped_ref, total_ref):
@@ -42,21 +43,16 @@
         def _():
             total_ref[...] = jnp.zeros_like(total_ref)
 
-        for group in range(block // 16):
-            picked = pl.ds(group * 16, 16)
-            flags = mask_ref[picked, :].astype(jnp.float32)
-            for row in range(rows):
-                values = sample_ref[picked, row * LANES : (row + 1) * LANES].astype(jnp.float32)
-                values = jnp.clip(values, -clip_level, clip_level) * flags[:, row : row + 1]
-                for half in range(2):
-                    part = values[8 * half : 8 * half + 8]
-                    first = (group * 16 + 8 * half) * 2 * rows + row
-                    wrapped_ref[pl.ds(first, 8, stride=2 * rows), :] = part
-                    wrapped_ref[pl.ds(first + rows, 8, stride=2 * rows), :] = part
+        flags = mask_ref[...]
+        for chan in range(block):
+            values = jnp.clip(sample_ref[chan].astype(jnp.float32), -clip_level, clip_level)
+            values = values * flags[:, chan : chan + 1]
+            wrapped_ref[chan * 2 * rows : chan * 2 * rows + rows, :] = values
+            wrapped_ref[chan * 2 * rows + rows : (chan + 1) * 2 * rows, :] = values
 
         lane = lax.broadcasted_iota(jnp.int32, (rows, LANES), 1)
         index = lax.broadcasted_iota(jnp.int32, (rows, LANES), 0) * LANES + lane
-        from_end = LANES - 1 - lane[:8]
+        from_end = LANES - 1 - lane[:16]
 
         def one_dm(dm, _):
             chan_base = dm * chan_count + step * block
@@ -68,14 +64,19 @@
                 start = chan * (2 * rows) + (rows - 1) - (delay >> lane_bits)
                 keep = from_end >= low
                 new_both, new_own = [], []
-                for r in range(rows // 8):
-                    same = wrapped_ref[pl.ds(start + (1 + 8 * r), 8), :]
-                    before = wrapped_ref[pl.ds(start + 8 * r, 8), :]
-                    moved = pltpu.roll(jnp.where(keep, same, before), low, 1)
-                    new_both.append(both[r] + moved)
-                    new_own.append(
-                        own[r] + jnp.where(index[8 * r : 8 * r + 8] >= delay, moved, 0.0)
-                    )
+                before = wrapped_ref[pl.ds(start, rows), :]
+                same = wrapped_ref[pl.ds(start + 1, rows), :]
+                for r in range(rows // 16):
+                    pair = slice(16 * r, 16 * r + 16)
+                    merged = jnp.where(keep, same[pair], before[pair]).astype(jnp.bfloat16)
+                    rolled = pltpu.roll(merged, low, 1).astype(jnp.float32)
+                    for h in range(2):
+                        moved = rolled[8 * h : 8 * h + 8]
+                        t = 2 * r + h
+                        new_both.append(both[t] + moved)
+                        new_own.append(
+                            own[t] + jnp.where(index[8 * t : 8 * t + 8] >= delay, moved, 0.0)
+                        )
                 return (tuple(new_both), tuple(new_own))
 
             tiles = [slice(8 * r, 8 * r + 8) for r in range(rows // 8)]
@@ -117,8 +118,8 @@
             num_scalar_prefetch=1,
             grid=(steps,),
             in_specs=[
-                pl.BlockSpec((block, slab_len), lambda i, *_: (i, 0)),
-                pl.BlockSpec((block, clip_mask.shape[1]), lambda i, *_: (i, 0)),
+                pl.BlockSpec((block, rows, LANES), lambda i, *_: (i, 0, 0)),
+                pl.BlockSpec((rows, block), lambda i, *_: (0, i)),
             ],
             out_specs=pl.BlockSpec((dm_count, 2 * rows, LANES), lambda i, *_: (0, 0, 0)),
             scratch_shapes=[
@@ -127,7 +128,11 @@
             ],
         ),
         compiler_params=pltpu.CompilerParams(vmem_limit_bytes=48 << 20),
-    )(delays.reshape(-1), samples, clip_mask)
+    )(
+        delays.reshape(-1),
+        samples.reshape(chan_count, rows, LANES),
+        clip_mask.T.astype(jnp.float32),
+    )
 
 
 def gather_series(partial_value):

time: 73.9 us -> 53.7 us (0.73)
  Pallas kernels: 65.2 us -> 44.6 us
    pallas_call x1, Pallas kernels: 44.6 us -> 23.8 us  [dedisperse(): pl.pallas_call(kernel, out_shape=jax.ShapeDtypeStruct((dm_count, 2 * rows...]
where the time goes in v2:
time: 53.7 us; the launch traced here: 53.4 us
  Pallas kernels  44.6 us (83%)
  local copies, waits for them, and re-layouts  5.02 us (9%)
  matrix products  1.85 us (3%)
  other arithmetic  1.79 us (3%)
    pallas_call x1, Pallas kernels, dedisperse(): pl.pallas_call(kernel, out_shape=jax.ShapeDtypeStruct((dm_count, 2 * rows...  23.8 us
    pallas_call x1, Pallas kernels, gather_series(): pl.pallas_call(kernel, out_shape=jax.ShapeDtypeStruct((tm_count * rows, L...  12.2 us
    pallas_call x1, Pallas kernels, correlate(): pl.pallas_call(kernel, out_shape=jax.ShapeDtypeStruct((1, tmpl_count, bin...  8.64 us
    unnamed x8, local copies, waits for them, and re-layouts  4.84 us
    dot_general x1, matrix products, search(): folded = jnp.dot(table_outer, whole, precision=highest)  1.6 us

profile of v2, /device:TPU:0, one launch (start us, length us, event | category | flops | bytes accessed | tf_op | source)
XLA Modules:
  0.0 53.4 jit_solution(15539065631121966121)
XLA Ops:
  0.0 0.7 %copy.5 = s32[1,4,8,128]{3,1,2,0:T(4,128)S(1)} copy(s32[1,4,8,128]{3,2,1,0:T(8,128)} %bitcast.12) | data formatting | bytes 32768
  0.7 0.0 copy-start.2
  0.7 3.5 %copy.6 = bf16[64,8,32,128]{3,2,1,0:T(8,128)(2,1)S(1)} copy(bf16[64,8,32,128]{3,1,2,0:T(8,128)(2,1)} %bitcast.10) | data formatting | bytes 8388608
  4.2 0.0 copy-start.1
  4.2 0.0 copy-done.2
  4.2 23.8 %shard_map.46.part_ref = bf16[8,64,128]{2,1,0:T(8,128)(2,1)S(1)} custom-call(s32[4096]{0:T(1024)S(1)} %bitcast.9, bf16[512,32,128]{2,1,0:T(8,128)(2,1)S(1)} %bitcast.8, f32[32,512]{1,0:T(8,128)S(1)} %convert_bitcast_fusion.mask_ref), custom_call_target="tpu_custom_call" | custom-call | tf_op jit(solution)/shard_map/pallas_call | solution.py:114
  28.0 0.0 copy-start
  28.1 0.6 %copy-done = bf16[8,64,128]{2,1,0:T(8,128)(2,1)} copy-done((bf16[8,64,128]{2,1,0:T(8,128)(2,1)}, bf16[8,64,128]{2,1,0:T(8,128)(2,1)S(1)}, u32[]{:S(2)}) %copy-start) | copy-done | bytes 131096
  28.7 12.2 %shard_map.47 = f32[256,128]{1,0:T(8,128)} custom-call(bf16[8,64,128]{2,1,0:T(8,128)(2,1)} %copy-done), custom_call_target="tpu_custom_call" | custom-call | tf_op jit(solution)/shard_map/pallas_call | solution.py:212
  40.9 1.0 %sine_negate_fusion = (f32[256,256]{1,0:T(8,128)S(1)}, f32[256,256]{1,0:T(8,128)S(1)}) fusion(), kind=kLoop, calls=%fused_computation.14 | loop fusion | flops 983040 | bytes 524288 | tf_op jit(solution)/shard_map/neg | solution.py:300
  41.9 1.6 %fusion = f32[512,128]{0,1:T(8,128)S(1)} fusion(f32[256,128]{1,0:T(8,128)} %shard_map.47, f32[256,256]{1,0:T(8,128)S(1)} %get-tuple-element.10, f32[256,256]{1,0:T(8,128)S(1)} %get-tuple-element.11), kind=kOutput, calls=%fused_computation | convolution fusion | flops 201457664 | bytes 917504 | tf_op jit(solution)/shard_map/dot_general | solution.py:303
  43.5 0.6 %multiply_add_fusion = (f32[256,128]{0,1:T(8,128)S(1)}, f32[256,128]{0,1:T(8,128)S(1)}) fusion(f32[512,128]{0,1:T(8,128)S(1)} %fusion), kind=kLoop, calls=%fused_computation.25 | loop fusion | flops 655360 | bytes 524288 | tf_op jit(solution)/shard_map/add | solution.py:306
  44.1 0.2 fusion.36
  44.3 0.3 fusion.7
  44.6 0.1 pad.4.framed_ref
  44.8 0.0 copy-done.1
  44.8 8.6 %shard_map.48 = f32[1,64,8192]{2,1,0:T(8,128)} custom-call(f32[2,9216]{1,0:T(2,128)S(1)} %pad.4.framed_ref, bf16[2,64,1024]{2,1,0:T(8,128)(2,1)S(1)} %copy-done.1), custom_call_target="tpu_custom_call" | custom-call | tf_op jit(solution)/shard_map/pallas_call | solution.py:271
  (4 shorter events, 0.1 us)
Async XLA Ops:
  0.7 3.5 %copy-start.2 = (s32[512,32]{0,1:T(8,128)S(1)}, s32[512,32]{0,1:T(8,128)}, u32[]{:S(2)}) copy-start(s32[512,32]{0,1:T(8,128)} %param.5) | copy-start | bytes 196612
  4.2 40.6 %copy-start.1 = (bf16[2,64,1024]{2,1,0:T(8,128)(2,1)S(1)}, bf16[2,64,1024]{2,1,0:T(8,128)(2,1)}, u32[]{:S(2)}) copy-start(bf16[2,64,1024]{2,1,0:T(8,128)(2,1)} %tmpl_ref.1) | copy-start | bytes 786436
  28.0 0.7 %copy-start = (bf16[8,64,128]{2,1,0:T(8,128)(2,1)}, bf16[8,64,128]{2,1,0:T(8,128)(2,1)S(1)}, u32[]{:S(2)}) copy-start(bf16[8,64,128]{2,1,0:T(8,128)(2,1)S(1)} %shard_map.46.part_ref) | copy-start | bytes 393220

commit v3 on v2

--- a/solution.py
+++ b/solution.py
@@ -12,7 +12,7 @@
 LANES = 128
 
 clip_level = 2.5
-highest = lax.Precision.HIGHEST
+fine = lax.Precision.HIGH
 
 
 def counting(length):
@@ -88,7 +88,7 @@
                     tuple(total_ref[dm, 0, t, :] for t in tiles),
                     tuple(total_ref[dm, 1, t, :] for t in tiles),
                 ),
-                unroll=64,
+                unroll=block,
             )
             for t, x, y in zip(tiles, both, own):
                 total_ref[dm, 0, t, :] = x
@@ -300,7 +300,7 @@
     table_outer = jnp.concatenate([outer_cos, -outer_sin], axis=0)
     hold_cos, hold_sin = phase_table(counting(row_count), counting(inner_len), total_len)
     own_cols = bin_cols // lax.axis_size("band")
-    folded = jnp.dot(table_outer, whole, precision=highest)
+    folded = jnp.dot(table_outer, whole, precision=fine)
     fold_real = folded[:row_count]
     fold_imag = folded[row_count:]
     hold_real = fold_real * hold_cos + fold_imag * hold_sin
@@ -319,7 +319,7 @@
         ],
         axis=0,
     )
-    out = jnp.dot(jnp.concatenate([hold_real, hold_imag], axis=1), table_last, precision=highest)
+    out = jnp.dot(jnp.concatenate([hold_real, hold_imag], axis=1), table_last, precision=fine)
     ordered = out.T.reshape(2, -1)
     local_bins = own_cols * row_count
     skip = side_cols * row_count - half_taps

time: 53.7 us -> 52.6 us (0.980)
  Pallas kernels: 44.6 us -> 43.9 us
    pallas_call x1, Pallas kernels: 23.8 us -> 23.3 us  [dedisperse(): pl.pallas_call(kernel, out_shape=jax.ShapeDtypeStruct((dm_count, 2 * rows...]
where the time goes in v3:
time: 52.6 us; the launch traced here: 52.3 us
  Pallas kernels  43.9 us (83%)
  local copies, waits for them, and re-layouts  5.02 us (10%)
  other arithmetic  1.79 us (3%)
  matrix products  1.54 us (3%)
    pallas_call x1, Pallas kernels, dedisperse(): pl.pallas_call(kernel, out_shape=jax.ShapeDtypeStruct((dm_count, 2 * rows...  23.3 us
    pallas_call x1, Pallas kernels, gather_series(): pl.pallas_call(kernel, out_shape=jax.ShapeDtypeStruct((tm_count * rows, L...  12.2 us
    pallas_call x1, Pallas kernels, correlate(): pl.pallas_call(kernel, out_shape=jax.ShapeDtypeStruct((1, tmpl_count, bin...  8.41 us
    unnamed x8, local copies, waits for them, and re-layouts  4.84 us
    dot_general x1, matrix products, search(): folded = jnp.dot(table_outer, whole, precision=fine)  1.32 us

profile of v3, /device:TPU:0, one launch (start us, length us, event | category | flops | bytes accessed | tf_op | source)
XLA Modules:
  0.0 52.3 jit_solution(13826376718982631405)
XLA Ops:
  0.0 0.7 %copy.5 = s32[1,4,8,128]{3,1,2,0:T(4,128)S(1)} copy(s32[1,4,8,128]{3,2,1,0:T(8,128)} %bitcast.12) | data formatting | bytes 32768
  0.7 0.0 copy-start.2
  0.7 3.5 %copy.6 = bf16[64,8,32,128]{3,2,1,0:T(8,128)(2,1)S(1)} copy(bf16[64,8,32,128]{3,1,2,0:T(8,128)(2,1)} %bitcast.10) | data formatting | bytes 8388608
  4.2 0.0 copy-start.1
  4.2 0.0 copy-done.2
  4.2 23.3 %shard_map.46.part_ref = bf16[8,64,128]{2,1,0:T(8,128)(2,1)S(1)} custom-call(s32[4096]{0:T(1024)S(1)} %bitcast.9, bf16[512,32,128]{2,1,0:T(8,128)(2,1)S(1)} %bitcast.8, f32[32,512]{1,0:T(8,128)S(1)} %convert_bitcast_fusion.mask_ref), custom_call_target="tpu_custom_call" | custom-call | tf_op jit(solution)/shard_map/pallas_call | solution.py:114
  27.5 0.0 copy-start
  27.5 0.6 %copy-done = bf16[8,64,128]{2,1,0:T(8,128)(2,1)} copy-done((bf16[8,64,128]{2,1,0:T(8,128)(2,1)}, bf16[8,64,128]{2,1,0:T(8,128)(2,1)S(1)}, u32[]{:S(2)}) %copy-start) | copy-done | bytes 131096
  28.2 12.2 %shard_map.47 = f32[256,128]{1,0:T(8,128)} custom-call(bf16[8,64,128]{2,1,0:T(8,128)(2,1)} %copy-done), custom_call_target="tpu_custom_call" | custom-call | tf_op jit(solution)/shard_map/pallas_call | solution.py:212
  40.3 1.0 %sine_negate_fusion = (f32[256,256]{1,0:T(8,128)S(1)}, f32[256,256]{1,0:T(8,128)S(1)}) fusion(), kind=kLoop, calls=%fused_computation.14 | loop fusion | flops 983040 | bytes 524288 | tf_op jit(solution)/shard_map/neg | solution.py:300
  41.4 1.3 %fusion = f32[512,128]{0,1:T(8,128)S(1)} fusion(f32[256,128]{1,0:T(8,128)} %shard_map.47, f32[256,256]{1,0:T(8,128)S(1)} %get-tuple-element.10, f32[256,256]{1,0:T(8,128)S(1)} %get-tuple-element.11), kind=kOutput, calls=%fused_computation | convolution fusion | flops 100794368 | bytes 917504 | tf_op jit(solution)/shard_map/dot_general | solution.py:303
  42.7 0.6 %multiply_add_fusion = (f32[256,128]{0,1:T(8,128)S(1)}, f32[256,128]{0,1:T(8,128)S(1)}) fusion(f32[512,128]{0,1:T(8,128)S(1)} %fusion), kind=kLoop, calls=%fused_computation.25 | loop fusion | flops 655360 | bytes 524288 | tf_op jit(solution)/shard_map/add | solution.py:306
  43.3 0.2 fusion.36
  43.5 0.2 fusion.7
  43.8 0.1 pad.4.framed_ref
  43.9 0.0 copy-done.1
  43.9 8.4 %shard_map.48 = f32[1,64,8192]{2,1,0:T(8,128)} custom-call(f32[2,9216]{1,0:T(2,128)S(1)} %pad.4.framed_ref, bf16[2,64,1024]{2,1,0:T(8,128)(2,1)S(1)} %copy-done.1), custom_call_target="tpu_custom_call" | custom-call | tf_op jit(solution)/shard_map/pallas_call | solution.py:271
  (4 shorter events, 0.1 us)
Async XLA Ops:
  0.7 3.5 %copy-start.2 = (s32[512,32]{0,1:T(8,128)S(1)}, s32[512,32]{0,1:T(8,128)}, u32[]{:S(2)}) copy-start(s32[512,32]{0,1:T(8,128)} %param.5) | copy-start | bytes 196612
  4.2 39.7 %copy-start.1 = (bf16[2,64,1024]{2,1,0:T(8,128)(2,1)S(1)}, bf16[2,64,1024]{2,1,0:T(8,128)(2,1)}, u32[]{:S(2)}) copy-start(bf16[2,64,1024]{2,1,0:T(8,128)(2,1)} %tmpl_ref.1) | copy-start | bytes 786436
  27.5 0.7 %copy-start = (bf16[8,64,128]{2,1,0:T(8,128)(2,1)}, bf16[8,64,128]{2,1,0:T(8,128)(2,1)S(1)}, u32[]{:S(2)}) copy-start(bf16[8,64,128]{2,1,0:T(8,128)(2,1)S(1)} %shard_map.46.part_ref) | copy-start | bytes 393220
